TPU v7x, 256 devices: a whole 4x4x8 slice. The times are simulated.
256 devices in a mesh: dp: 16 (over x, y), expert: 16 (over z, core).
Axes of the slice: x: 4, y: 4, z: 8, core: 2. Of those that a mesh axis runs over, the one named last changes fastest.
Arguments:
- hidden: bfloat16 [16, 16, 384, 1024], P('dp', 'expert'), may hold values from -6 to 6
- down_weight: bfloat16 [16, 1024, 3584], P('expert'), may hold values from -0.1875 to 0.1875
- cotangent: bfloat16 [8192, 3584], P('dp', 'expert'), may hold values from -6 to 6
- expert_ids: int32 [8192, 8], P('dp'), may hold values from 0 to 15, as said below
- gate_weights: bfloat16 [8192, 8], P('dp'), may hold values from 0.049804688 to 0.5
- row_token: int32 [16, 16, 384], P('dp', 'expert'), may hold values from -1 to 511, as said below
- tile_count: int32 [16, 16], P('dp', 'expert'), may hold values from 1 to 3, as said below
Outputs:
- mixed_out: bfloat16 [8192, 3584], P('dp', 'expert')
- hidden_grad: bfloat16 [16, 16, 384, 1024], P('dp', 'expert')
- weight_grad: float32 [16, 1024, 3584], P('expert', 'dp')
Inputs may be any that keep to these rules, and one draw needn't show every extreme that they name: `expert_ids`: each token names 8 different experts; every expert is named by some token of every group. row_token[i, e, r] is the index within group i (0 to 511) of a token that names expert e, or -1 for an empty slot; each token of a group stands exactly once in the rows of each expert it names and nowhere else; an expert's filled rows come first. tile_count[i, e] is the number of 128-row tiles that hold expert e's filled rows in group i, except for one expert of every group whose count is one tile less; the busiest expert of every group has 384 filled rows, all of them counted.
All inputs are finite; a program needn't handle non-finite values.
Results may differ from a plain program's by a relative error of at most 0.013.
Values may be sent and summed in bfloat16 or wider, within the bound.
A program may use at most 128 MiB of HBM per device.

v0:
```python
import jax
import jax.numpy as jnp
from jax import lax
from jax.sharding import PartitionSpec as P

EXPERTS = 16
TILE = 128


def swapped(shard, axis, bit):
    return lax.ppermute(shard, axis, [(i, i ^ 1 << bit) for i in range(lax.axis_size(axis))])


def tile_products(rows_in, weight_mat, count, contract_dim):
    rows_cap = rows_in.shape[0]
    width_out = weight_mat.shape[1 - contract_dim]

    def one_tile(tile_index, outputs):
        block = lax.dynamic_slice_in_dim(rows_in, tile_index * TILE, TILE, 0)
        product = lax.dot_general(
            block,
            weight_mat,
            (((1,), (contract_dim,)), ((), ())),
            preferred_element_type=jnp.float32,
        )
        return lax.dynamic_update_slice_in_dim(
            outputs, product.astype(jnp.bfloat16), tile_index * TILE, 0
        )

    return lax.fori_loop(0, count, one_tile, jnp.zeros((rows_cap, width_out), jnp.bfloat16))


def body(hidden, down_weight, cotangent, expert_ids, gate_weights, row_token, tile_count):
    local_count = down_weight.shape[0]
    group_size = cotangent.shape[0]
    expert_index = jnp.arange(EXPERTS, dtype=jnp.int32)
    named_cols = expert_ids[:, :, None] == expert_index[None, None, :]
    gate_cols = jnp.sum(
        jnp.where(named_cols, gate_weights[:, :, None].astype(jnp.float32), 0.0), axis=1
    ).astype(jnp.bfloat16)
    group_cot = lax.all_gather(cotangent, "expert", axis=1, tiled=True)
    width = group_cot.shape[1]
    first_expert = lax.axis_index("expert") * local_count
    slot_index = jnp.arange(hidden.shape[2], dtype=jnp.int32)
    share_rows = down_weight.shape[1] // lax.axis_size("dp")
    partial_value = jnp.zeros((group_size, width), jnp.float32)
    token_rows = row_token[0, 0]
    count = tile_count[0, 0]
    live_rows = (token_rows >= 0) & (slot_index < count * TILE)
    safe_rows = jnp.where(live_rows, token_rows, 0)
    column = lax.dynamic_index_in_dim(gate_cols, first_expert + 0, 1, keepdims=False)
    row_gate = jnp.where(live_rows, column[safe_rows].astype(jnp.float32), 0.0)
    target = jnp.where(live_rows, token_rows, group_size)
    hidden_rows = hidden[0, 0]
    weight_mat = down_weight[0]
    out_rows = tile_products(hidden_rows, weight_mat, count, 0)
    partial_value = partial_value.at[target].add(
        row_gate[:, None] * out_rows.astype(jnp.float32), mode="drop"
    )
    routed = (row_gate[:, None] * group_cot[safe_rows].astype(jnp.float32)).astype(jnp.bfloat16)
    grad_list = [tile_products(routed, weight_mat, count, 1)]

    def weight_rows(start, rows_count, hidden_rows=hidden_rows, routed_rows=routed):
        return lax.dot_general(
            hidden_rows, routed_rows, (((0,), (0,)), ((), ())), preferred_element_type=jnp.float32
        )

    weight_list = [
        lax.psum_scatter(
            weight_rows(jnp.int32(0), share_rows * lax.axis_size("dp")).astype(jnp.bfloat16),
            "dp",
            scatter_dimension=0,
            tiled=True,
        ).astype(jnp.float32)
    ]
    merged = partial_value
    top_bit = lax.axis_size("expert").bit_length() - 1
    axis_index = lax.axis_index("expert")
    for bit_index in reversed(range(top_bit)):
        half_cols = merged.shape[1] // 2
        lower_half = merged[:, :half_cols]
        upper_half = merged[:, half_cols:]
        high_side = axis_index // 2**bit_index % 2 == 1
        sending = jnp.where(high_side, lower_half, upper_half)
        keeping = jnp.where(high_side, upper_half, lower_half)
        merged = keeping + swapped(sending.astype(jnp.bfloat16), "expert", bit_index).astype(
            sending.dtype
        )
    mixed_out = merged.astype(jnp.bfloat16)
    hidden_grad = jnp.stack(grad_list, axis=0)[None]
    weight_grad = jnp.stack(weight_list, axis=0)
    return (mixed_out, hidden_grad, weight_grad)


def solution(mesh):
    placed = (
        P("dp", "expert", None, None),
        P("expert", None, None),
        P("dp", "expert"),
        P("dp", None),
        P("dp", None),
        P("dp", "expert", None),
        P("dp", "expert"),
    )
    return jax.shard_map(
        body,
        mesh=mesh,
        in_specs=placed,
        out_specs=(P("dp", "expert"), P("dp", "expert", None, None), P("expert", "dp", None)),
        check_vma=False,
    )
```

profile of v0, /device:TPU:1, one launch (start us, length us, event | category | flops | bytes accessed | tf_op | source)
XLA Modules:
  0.0 314.3 jit_solution(3200420147319569231)
XLA Ops:
  10.8 2.8 gather_fusion
  14.3 41.0 %all-gather.2.cloned.1.call-done = bf16[512,3584]{0,1:T(8,128)(2,1)} async-done(((bf16[512,224]{0,1:T(8,128)(2,1)}), bf16[512,3584]{0,1:T(8,128)(2,1)}) %all-gather.2.cloned.1.call-update) | async-done | bytes 3670032 | tf_op jit(solution)/shard_map/all_gather | solution.py:41
  55.3 6.0 %copy.24 = bf16[512,3584]{1,0:T(8,128)(2,1)} copy(bf16[512,3584]{0,1:T(8,128)(2,1)} %all-gather.2.cloned.1.call-done) | data formatting | bytes 7340032 | tf_op jit(solution)/shard_map/all_gather | solution.py:41
  61.3 10.1 %gather_fusion.1 = bf16[384,3584]{1,0:T(8,128)(2,1)} fusion(bf16[512,3584]{1,0:T(8,128)(2,1)} %copy.24, s32[1024]{0:T(1024)S(1)} %pad_clamp_fusion), kind=kCustom, calls=%fused_computation.1 | custom fusion | bytes 5506560 | tf_op jit(solution)/shard_map/gather | solution.py:60
  71.4 2.6 multiply_convert_fusion
  74.1 6.2 %fusion.6 = bf16[1024,3584]{0,1:T(8,128)(2,1)} fusion(bf16[384,3584]{1,0:T(8,128)(2,1)S(1)} %multiply_convert_fusion, bf16[1,1,384,1024]{3,2,1,0:T(8,128)(2,1)S(1)} %copy-done.3), kind=kOutput, calls=%fused_computation.12 | convolution fusion | flops 2822242304 | bytes 10878976 | tf_op jit(solution)/shard_map/dot_general | solution.py:64
  80.2 10.0 %copy.27 = bf16[1024,3584]{1,0:T(8,128)(2,1)} copy(bf16[1024,3584]{0,1:T(8,128)(2,1)} %fusion.6) | data formatting | bytes 14680064
  92.0 18.8 %while.20 = (s32[]{:T(128)}, bf16[384,3584]{1,0:T(8,128)(2,1)}, s32[]{:T(128)}, bf16[384,1024]{1,0:T(8,128)(2,1)S(1)}, bf16[1024,3584]{1,0:T(8,128)(2,1)}, /*index=5*/s32[]{:T(128)}, s32[]{:T(128)}, s32[]{:T(128)}, s32[]{:T(128)}) while((s32[]{:T(128)}, bf16[384,3584]{1,0:T(8,128)(2,1)}, s32[]{:T(128)}, bf16[384,1024]{1,0:T(8,128)(2,1)S(1)}, ...), condition=%wide.region_2.3_spmd, body=%wide.region_1.2_spmd.sunk | while | flops 939982848 | bytes 8520843 | solution.py:30
  92.7 5.1 %fusion.28 = bf16[384,3584]{1,0:T(8,128)(2,1)} fusion(bf16[384,3584]{1,0:T(8,128)(2,1)} %get-tuple-element.169, s32[]{:T(128)S(6)} %select_n.202, bf16[1024,3584]{1,0:T(8,128)(2,1)} %get-tuple-element.181, bf16[384,1024]{1,0:T(8,128)(2,1)S(1)} %get-tuple-element.180), kind=kOutput, calls=%fused_computation.4.clone.1 | convolution fusion | flops 939982848 | bytes 8520704 | tf_op jit(solution)/shard_map/while/body/dot_general | solution.py:20
  98.5 5.5 %fusion.28 = bf16[384,3584]{1,0:T(8,128)(2,1)} fusion(bf16[384,3584]{1,0:T(8,128)(2,1)} %get-tuple-element.169, s32[]{:T(128)S(6)} %select_n.202, bf16[1024,3584]{1,0:T(8,128)(2,1)} %get-tuple-element.181, bf16[384,1024]{1,0:T(8,128)(2,1)S(1)} %get-tuple-element.180), kind=kOutput, calls=%fused_computation.4.clone.1 | convolution fusion | flops 939982848 | bytes 8520704 | tf_op jit(solution)/shard_map/while/body/dot_general | solution.py:20
  104.6 5.3 %fusion.28 = bf16[384,3584]{1,0:T(8,128)(2,1)} fusion(bf16[384,3584]{1,0:T(8,128)(2,1)} %get-tuple-element.169, s32[]{:T(128)S(6)} %select_n.202, bf16[1024,3584]{1,0:T(8,128)(2,1)} %get-tuple-element.181, bf16[384,1024]{1,0:T(8,128)(2,1)S(1)} %get-tuple-element.180), kind=kOutput, calls=%fused_computation.4.clone.1 | convolution fusion | flops 939982848 | bytes 8520704 | tf_op jit(solution)/shard_map/while/body/dot_general | solution.py:20
  110.8 12.9 %scatter_custom_fusion = f32[512,3584]{1,0:T(8,128)} fusion(s32[384]{0:T(512)S(1)} %get-tuple-element.74, bf16[384,3584]{1,0:T(8,128)(2,1)} %get-tuple-element.59, f32[]{:T(128)} %constant.98.clone.1, f32[384]{0:T(512)S(1)} %convert_select_fusion), kind=kCustom, calls=%fused_computation.14 | custom fusion | flops 4128768 | bytes 10094596 | tf_op jit(solution)/shard_map/scatter-add | solution.py:57
  123.6 4.9 %select_convert_fusion = bf16[512,1792]{1,0:T(8,128)(2,1)} fusion(f32[512,3584]{1,0:T(8,128)} %scatter_custom_fusion, pred[]{:T(512)S(6)} %eq.33), kind=kLoop, calls=%fused_computation.18 | loop fusion | flops 917504 | bytes 5505025 | tf_op jit(solution)/shard_map/convert_element_type | solution.py:86
  128.6 80.4 %collective-permute-done = bf16[512,1792]{1,0:T(8,128)(2,1)} collective-permute-done((bf16[512,1792]{1,0:T(8,128)(2,1)}, bf16[512,1792]{1,0:T(8,128)(2,1)}, u32[]{:S(2)}, u32[]{:S(2)}) %collective-permute-start) | collective-permute-done | bytes 1835040 | tf_op jit(solution)/shard_map/ppermute | solution.py:11
  209.0 4.3 %convert_add_fusion = f32[512,1792]{1,0:T(8,128)S(1)} fusion(bf16[512,1792]{1,0:T(8,128)(2,1)} %collective-permute-done, f32[512,3584]{1,0:T(8,128)} %scatter_custom_fusion, pred[]{:T(512)S(6)} %eq.33), kind=kLoop, calls=%fused_computation.17 | loop fusion | flops 2752512 | bytes 12845057 | tf_op jit(solution)/shard_map/add | solution.py:86
  213.2 1.9 copy-done
  216.2 43.0 %collective-permute-done.1 = bf16[512,896]{1,0:T(8,128)(2,1)} collective-permute-done((bf16[512,896]{1,0:T(8,128)(2,1)}, bf16[512,896]{1,0:T(8,128)(2,1)}, u32[]{:S(2)}, u32[]{:S(2)}) %collective-permute-start.1) | collective-permute-done | bytes 917536 | tf_op jit(solution)/shard_map/ppermute | solution.py:11
  259.2 2.6 convert_add_fusion.1
  263.6 13.1 %collective-permute-done.2 = bf16[512,448]{1,0:T(8,128)(2,1)} collective-permute-done((bf16[512,448]{1,0:T(8,128)(2,1)S(1)}, bf16[512,448]{1,0:T(8,128)(2,1)}, u32[]{:S(2)}, u32[]{:S(2)}) %collective-permute-start.2) | collective-permute-done | bytes 458784 | tf_op jit(solution)/shard_map/ppermute | solution.py:11
  276.7 2.0 convert_add_fusion.2
  284.9 19.3 %while.21 = (s32[]{:T(128)}, bf16[384,1024]{1,0:T(8,128)(2,1)S(1)}, s32[]{:T(128)}, bf16[384,3584]{1,0:T(8,128)(2,1)S(1)}, bf16[1024,3584]{1,0:T(8,128)(2,1)}, /*index=5*/s32[]{:T(128)}, s32[]{:T(128)}, s32[]{:T(128)}, s32[]{:T(128)}) while((s32[]{:T(128)}, bf16[384,1024]{1,0:T(8,128)(2,1)S(1)}, s32[]{:T(128)}, ...), condition=%wide.region_5.6_spmd, body=%wide.region_4.5_spmd.sunk | while | flops 939655168 | bytes 8520843 | solution.py:30
  285.5 5.5 %fusion.31 = bf16[384,1024]{1,0:T(8,128)(2,1)S(1)} fusion(bf16[384,1024]{1,0:T(8,128)(2,1)S(1)} %get-tuple-element.196, s32[]{:T(128)S(6)} %select_n.203, bf16[1024,3584]{1,0:T(8,128)(2,1)} %get-tuple-element.208, bf16[384,3584]{1,0:T(8,128)(2,1)S(1)} %get-tuple-element.207), kind=kOutput, calls=%fused_computation.8.clone.1 | convolution fusion | flops 939655168 | bytes 8520704 | tf_op jit(solution)/shard_map/while/body/dot_general | solution.py:20
  291.7 5.5 %fusion.31 = bf16[384,1024]{1,0:T(8,128)(2,1)S(1)} fusion(bf16[384,1024]{1,0:T(8,128)(2,1)S(1)} %get-tuple-element.196, s32[]{:T(128)S(6)} %select_n.203, bf16[1024,3584]{1,0:T(8,128)(2,1)} %get-tuple-element.208, bf16[384,3584]{1,0:T(8,128)(2,1)S(1)} %get-tuple-element.207), kind=kOutput, calls=%fused_computation.8.clone.1 | convolution fusion | flops 939655168 | bytes 8520704 | tf_op jit(solution)/shard_map/while/body/dot_general | solution.py:20
  297.9 5.5 %fusion.31 = bf16[384,1024]{1,0:T(8,128)(2,1)S(1)} fusion(bf16[384,1024]{1,0:T(8,128)(2,1)S(1)} %get-tuple-element.196, s32[]{:T(128)S(6)} %select_n.203, bf16[1024,3584]{1,0:T(8,128)(2,1)} %get-tuple-element.208, bf16[384,3584]{1,0:T(8,128)(2,1)S(1)} %get-tuple-element.207), kind=kOutput, calls=%fused_computation.8.clone.1 | convolution fusion | flops 939655168 | bytes 8520704 | tf_op jit(solution)/shard_map/while/body/dot_general | solution.py:20
  (36 shorter events, 17.7 us)
Async XLA Ops:
  7.2 48.1 %all-gather.2.cloned.1.call-start = ((), (), s32[]{:S(2)}) async-start(), calls=%async_computation.1 | async-start | bytes 3899392 | tf_op jit(solution)/shard_map/all_gather | solution.py:41
  7.9 296.3 %reduce-scatter.4.cloned.1.call-start = ((), (), s32[]{:S(2)}) async-start(), calls=%async_computation.2 | async-start | bytes 7798784
  71.4 2.7 copy-start.3
  128.6 80.4 %collective-permute-start = (bf16[512,1792]{1,0:T(8,128)(2,1)}, bf16[512,1792]{1,0:T(8,128)(2,1)}, u32[]{:S(2)}, u32[]{:S(2)}) collective-permute-start(bf16[512,1792]{1,0:T(8,128)(2,1)} %select_convert_fusion), channel_id=1, source_target_pairs={{0,8},{1,9},{2,10},{3,11},{4,12},{5,13},{6,14},{7,15},{8,0},{9,1},... | collective-permute-start | bytes 5505032 | tf_op jit(solution)/shard_map/ppermute | solution.py:11
  213.2 1.9 copy-start
  216.2 43.0 %collective-permute-start.1 = (bf16[512,896]{1,0:T(8,128)(2,1)}, bf16[512,896]{1,0:T(8,128)(2,1)}, u32[]{:S(2)}, u32[]{:S(2)}) collective-permute-start(bf16[512,896]{1,0:T(8,128)(2,1)} %select_convert_fusion.1), channel_id=1, source_target_pairs={{0,4},{1,5},{2,6},{3,7},{4,0},{5,1},{6,2},{7,3},{8,12},{9,13},{10,... | collective-permute-start | bytes 2752520 | tf_op jit(solution)/shard_map/ppermute | solution.py:11
  261.8 1.3 copy-start.1
  263.3 13.4 %collective-permute-start.2 = (bf16[512,448]{1,0:T(8,128)(2,1)S(1)}, bf16[512,448]{1,0:T(8,128)(2,1)}, u32[]{:S(2)}, u32[]{:S(2)}) collective-permute-start(bf16[512,448]{1,0:T(8,128)(2,1)S(1)} %select_convert_fusion.2), channel_id=1, source_target_pairs={{0,2},{1,3},{2,0},{3,1},{4,6},{5,7},{6,4},{7,5},{8,10},{9,11},{10,... | collective-permute-start | bytes 1376264 | tf_op jit(solution)/shard_map/ppermute | solution.py:11
  278.7 1.0 copy-start.2
  279.9 2.6 collective-permute-start.3
  304.1 3.3 %copy-start.4 = (bf16[384,1024]{1,0:T(8,128)(2,1)}, bf16[384,1024]{1,0:T(8,128)(2,1)S(1)}, u32[]{:S(2)}) copy-start(bf16[384,1024]{1,0:T(8,128)(2,1)S(1)} %get-tuple-element.60) | copy-start | bytes 2359300
Sparse Core Ops, SparseCore 0:
  9.8 45.4 all-gather.1
  90.4 85.8 reduce-scatter.3
where the time goes:
time: 315 us; the launch traced here: 314 us
  waiting for transfers between devices  179 us (57%)
  local copies, waits for them, and re-layouts  38.9 us (12%)
  matrix products  38.7 us (12%)
  other arithmetic  35.2 us (11%)
  between operations  14.9 us (5%)
  loops' own time  5.51 us (2%)
    ppermute x4, waiting for transfers between devices, swapped(): lax.ppermute(shard, axis, [(i, i ^ 1 << bit) for i in range(lax.axis_size...  138 us
    all_gather x1, waiting for transfers between devices, body(): group_cot = lax.all_gather(cotangent, 'expert', axis=1, tiled=True)  41 us
    dot_general x6, matrix products, one_tile(): lax.dot_general(block, weight_mat, (((1,), (contract_dim,)), ((), ())), p...  32.5 us
    unnamed x14, local copies, waits for them, and re-layouts  18.2 us
    scatter-add x1, other arithmetic, body(): partial_value.at[target]  12.9 us
    gather x1, local copies, waits for them, and re-layouts, body(): group_cot[safe_rows].astype(jnp.float32)  10.1 us
    add x3, other arithmetic, body(): keeping + swapped(sending.astype(jnp.bfloat16), 'expert', bit_index).asty...  8.84 us
    convert_element_type x4, other arithmetic, body(): sending.astype(jnp.bfloat16)  6.37 us
  transfers between devices with their start and end apart: 6, of which 5 were waited for; matrix products, arithmetic and copies ran while one was open for 22% of the time, Pallas kernels for 0%

commit v1 on v0

--- a/solution.py
+++ b/solution.py
@@ -38,7 +38,10 @@
     gate_cols = jnp.sum(
         jnp.where(named_cols, gate_weights[:, :, None].astype(jnp.float32), 0.0), axis=1
     ).astype(jnp.bfloat16)
-    group_cot = lax.all_gather(cotangent, "expert", axis=1, tiled=True)
+    devices = lax.axis_size("expert")
+    pieces = jnp.stack([cotangent for _ in range(devices)])
+    pieces = lax.all_to_all(pieces, "expert", split_axis=0, concat_axis=0)
+    group_cot = jnp.concatenate(pieces, axis=1)
     width = group_cot.shape[1]
     first_expert = lax.axis_index("expert") * local_count
     slot_index = jnp.arange(hidden.shape[2], dtype=jnp.int32)

time: 315 us -> 363 us (1.15)
  waiting for transfers between devices: 179 us -> 215 us
  starting transfers between devices: 1.83 us -> 11.9 us
    all_to_all x0 -> x1, waiting for transfers between devices: none -> 78.6 us  [body(): pieces = lax.all_to_all(pieces, 'expert', split_axis=0, concat_axis=0)]
    all_gather x1 -> x0, waiting for transfers between devices: 41 us -> none  [body(): group_cot = lax.all_gather(cotangent, 'expert', axis=1, tiled=True)]
    all_to_all x0 -> x1, starting transfers between devices: none -> 10.1 us  [body(): pieces = lax.all_to_all(pieces, 'expert', split_axis=0, concat_axis=0)]
    all_gather x1 -> x0, local copies, waits for them, and re-layouts: 5.95 us -> none  [body(): group_cot = lax.all_gather(cotangent, 'expert', axis=1, tiled=True)]
    reshape x0 -> x1, local copies, waits for them, and re-layouts: none -> 5.92 us  [body(): group_cot = jnp.concatenate(pieces, axis=1)]
    unnamed x14 -> x20, local copies, waits for them, and re-layouts: 18.2 us -> 18.2 us
  transfers between devices with their start and end apart: 6 -> 6, of which waited for: 5 -> 5; matrix products, arithmetic and copies ran while one was open for 22% -> 19% of each run, Pallas kernels for 0% -> 0%
where the time goes in v1:
time: 363 us; the launch traced here: 360 us
  waiting for transfers between devices  215 us (59%)
  local copies, waits for them, and re-layouts  41.9 us (12%)
  matrix products  38.3 us (11%)
  other arithmetic  32.7 us (9%)
  between operations  14.9 us (4%)
  starting transfers between devices  11.9 us (3%)
  loops' own time  5.51 us (2%)
    ppermute x4, waiting for transfers between devices, swapped(): lax.ppermute(shard, axis, [(i, i ^ 1 << bit) for i in range(lax.axis_size...  136 us
    all_to_all x1, waiting for transfers between devices, body(): pieces = lax.all_to_all(pieces, 'expert', split_axis=0, concat_axis=0)  78.6 us
    dot_general x6, matrix products, one_tile(): lax.dot_general(block, weight_mat, (((1,), (contract_dim,)), ((), ())), p...  32.1 us
    unnamed x20, local copies, waits for them, and re-layouts  18.2 us
    scatter-add x1, other arithmetic, body(): partial_value.at[target]  12.8 us
    all_to_all x1, starting transfers between devices, body(): pieces = lax.all_to_all(pieces, 'expert', split_axis=0, concat_axis=0)  10.1 us
    gather x1, local copies, waits for them, and re-layouts, body(): group_cot[safe_rows].astype(jnp.float32)  10.1 us
    add x3, other arithmetic, body(): keeping + swapped(sending.astype(jnp.bfloat16), 'expert', bit_index).asty...  8.84 us
  transfers between devices with their start and end apart: 6, of which 5 were waited for; matrix products, arithmetic and copies ran while one was open for 19% of the time, Pallas kernels for 0%

profile of v1, /device:TPU:1, one launch (start us, length us, event | category | flops | bytes accessed | tf_op | source)
XLA Modules:
  0.0 360.3 jit_solution(10277565753340371572)
XLA Ops:
  7.2 3.1 stack.7
  10.3 10.1 %all-to-all-start = ((bf16[16,512,224]{1,2,0:T(8,128)(2,1)}), bf16[16,512,224]{1,2,0:T(8,128)(2,1)}, u32[]{:S(2)}, u32[]{:S(2)}) async-start(bf16[16,512,224]{1,2,0:T(8,128)(2,1)} %stack.7), calls=%async_computation | async-start | bytes 7340032 | tf_op jit(solution)/shard_map/all_to_all | solution.py:43
  21.2 2.8 gather_fusion
  24.1 78.6 %all-to-all-done = bf16[16,512,224]{1,2,0:T(8,128)(2,1)} async-done(((bf16[16,512,224]{1,2,0:T(8,128)(2,1)}), bf16[16,512,224]{1,2,0:T(8,128)(2,1)}, u32[]{:S(2)}, u32[]{:S(2)}) %all-to-all-start) | async-done | bytes 3670048 | tf_op jit(solution)/shard_map/all_to_all | solution.py:43
  102.7 5.9 %copy.24 = bf16[512,3584]{1,0:T(8,128)(2,1)} copy(bf16[512,3584]{0,1:T(8,128)(2,1)} %bitcast.5) | data formatting | bytes 7340032 | tf_op jit(solution)/shard_map/reshape | solution.py:44
  108.6 10.1 %gather_fusion.1 = bf16[384,3584]{1,0:T(8,128)(2,1)} fusion(bf16[512,3584]{1,0:T(8,128)(2,1)} %copy.24, s32[1024]{0:T(1024)S(1)} %pad_clamp_fusion), kind=kCustom, calls=%fused_computation.1 | custom fusion | bytes 5506560 | tf_op jit(solution)/shard_map/gather | solution.py:63
  118.7 2.6 multiply_convert_fusion
  121.4 6.2 %fusion.6 = bf16[1024,3584]{0,1:T(8,128)(2,1)} fusion(bf16[384,3584]{1,0:T(8,128)(2,1)S(1)} %multiply_convert_fusion, bf16[1,1,384,1024]{3,2,1,0:T(8,128)(2,1)S(1)} %copy-done.3), kind=kOutput, calls=%fused_computation.12 | convolution fusion | flops 2822242304 | bytes 10878976 | tf_op jit(solution)/shard_map/dot_general | solution.py:67
  127.5 10.0 %copy.27 = bf16[1024,3584]{1,0:T(8,128)(2,1)} copy(bf16[1024,3584]{0,1:T(8,128)(2,1)} %fusion.6) | data formatting | bytes 14680064
  139.3 18.4 %while.20 = (s32[]{:T(128)}, bf16[384,3584]{1,0:T(8,128)(2,1)}, s32[]{:T(128)}, bf16[384,1024]{1,0:T(8,128)(2,1)S(1)}, bf16[1024,3584]{1,0:T(8,128)(2,1)}, /*index=5*/s32[]{:T(128)}, s32[]{:T(128)}, s32[]{:T(128)}, s32[]{:T(128)}) while((s32[]{:T(128)}, bf16[384,3584]{1,0:T(8,128)(2,1)}, s32[]{:T(128)}, bf16[384,1024]{1,0:T(8,128)(2,1)S(1)}, ...), condition=%wide.region_2.3_spmd, body=%wide.region_1.2_spmd.sunk | while | flops 939982848 | bytes 8520843 | solution.py:30
  140.0 5.1 %fusion.28 = bf16[384,3584]{1,0:T(8,128)(2,1)} fusion(bf16[384,3584]{1,0:T(8,128)(2,1)} %get-tuple-element.169, s32[]{:T(128)S(6)} %select_n.202, bf16[1024,3584]{1,0:T(8,128)(2,1)} %get-tuple-element.181, bf16[384,1024]{1,0:T(8,128)(2,1)S(1)} %get-tuple-element.180), kind=kOutput, calls=%fused_computation.4.clone.1 | convolution fusion | flops 939982848 | bytes 8520704 | tf_op jit(solution)/shard_map/while/body/dot_general | solution.py:20
  145.8 5.2 %fusion.28 = bf16[384,3584]{1,0:T(8,128)(2,1)} fusion(bf16[384,3584]{1,0:T(8,128)(2,1)} %get-tuple-element.169, s32[]{:T(128)S(6)} %select_n.202, bf16[1024,3584]{1,0:T(8,128)(2,1)} %get-tuple-element.181, bf16[384,1024]{1,0:T(8,128)(2,1)S(1)} %get-tuple-element.180), kind=kOutput, calls=%fused_computation.4.clone.1 | convolution fusion | flops 939982848 | bytes 8520704 | tf_op jit(solution)/shard_map/while/body/dot_general | solution.py:20
  151.6 5.2 %fusion.28 = bf16[384,3584]{1,0:T(8,128)(2,1)} fusion(bf16[384,3584]{1,0:T(8,128)(2,1)} %get-tuple-element.169, s32[]{:T(128)S(6)} %select_n.202, bf16[1024,3584]{1,0:T(8,128)(2,1)} %get-tuple-element.181, bf16[384,1024]{1,0:T(8,128)(2,1)S(1)} %get-tuple-element.180), kind=kOutput, calls=%fused_computation.4.clone.1 | convolution fusion | flops 939982848 | bytes 8520704 | tf_op jit(solution)/shard_map/while/body/dot_general | solution.py:20
  157.7 12.8 %scatter_custom_fusion = f32[512,3584]{1,0:T(8,128)} fusion(s32[384]{0:T(512)S(1)} %get-tuple-element.74, bf16[384,3584]{1,0:T(8,128)(2,1)} %get-tuple-element.59, f32[]{:T(128)} %constant.98.clone.1, f32[384]{0:T(512)S(1)} %convert_select_fusion), kind=kCustom, calls=%fused_computation.14 | custom fusion | flops 4128768 | bytes 10094596 | tf_op jit(solution)/shard_map/scatter-add | solution.py:60
  170.5 5.2 %select_convert_fusion = bf16[512,1792]{1,0:T(8,128)(2,1)} fusion(f32[512,3584]{1,0:T(8,128)} %scatter_custom_fusion, pred[]{:T(512)S(6)} %eq.33), kind=kLoop, calls=%fused_computation.18 | loop fusion | flops 917504 | bytes 5505025 | tf_op jit(solution)/shard_map/convert_element_type | solution.py:89
  175.7 80.9 %collective-permute-done = bf16[512,1792]{1,0:T(8,128)(2,1)} collective-permute-done((bf16[512,1792]{1,0:T(8,128)(2,1)}, bf16[512,1792]{1,0:T(8,128)(2,1)}, u32[]{:S(2)}, u32[]{:S(2)}) %collective-permute-start) | collective-permute-done | bytes 1835040 | tf_op jit(solution)/shard_map/ppermute | solution.py:11
  256.6 4.3 %convert_add_fusion = f32[512,1792]{1,0:T(8,128)S(1)} fusion(bf16[512,1792]{1,0:T(8,128)(2,1)} %collective-permute-done, f32[512,3584]{1,0:T(8,128)} %scatter_custom_fusion, pred[]{:T(512)S(6)} %eq.33), kind=kLoop, calls=%fused_computation.17 | loop fusion | flops 2752512 | bytes 12845057 | tf_op jit(solution)/shard_map/add | solution.py:89
  263.9 41.3 %collective-permute-done.1 = bf16[512,896]{1,0:T(8,128)(2,1)} collective-permute-done((bf16[512,896]{1,0:T(8,128)(2,1)}, bf16[512,896]{1,0:T(8,128)(2,1)}, u32[]{:S(2)}, u32[]{:S(2)}) %collective-permute-start.1) | collective-permute-done | bytes 917536 | tf_op jit(solution)/shard_map/ppermute | solution.py:11
  305.1 2.6 convert_add_fusion.1
  309.6 13.1 %collective-permute-done.2 = bf16[512,448]{1,0:T(8,128)(2,1)} collective-permute-done((bf16[512,448]{1,0:T(8,128)(2,1)S(1)}, bf16[512,448]{1,0:T(8,128)(2,1)}, u32[]{:S(2)}, u32[]{:S(2)}) %collective-permute-start.2) | collective-permute-done | bytes 458784 | tf_op jit(solution)/shard_map/ppermute | solution.py:11
  330.8 19.3 %while.21 = (s32[]{:T(128)}, bf16[384,1024]{1,0:T(8,128)(2,1)S(1)}, s32[]{:T(128)}, bf16[384,3584]{1,0:T(8,128)(2,1)S(1)}, bf16[1024,3584]{1,0:T(8,128)(2,1)}, /*index=5*/s32[]{:T(128)}, s32[]{:T(128)}, s32[]{:T(128)}, s32[]{:T(128)}) while((s32[]{:T(128)}, bf16[384,1024]{1,0:T(8,128)(2,1)S(1)}, s32[]{:T(128)}, ...), condition=%wide.region_5.6_spmd, body=%wide.region_4.5_spmd.sunk | while | flops 939655168 | bytes 8520843 | solution.py:30
  331.5 5.5 %fusion.31 = bf16[384,1024]{1,0:T(8,128)(2,1)S(1)} fusion(bf16[384,1024]{1,0:T(8,128)(2,1)S(1)} %get-tuple-element.196, s32[]{:T(128)S(6)} %select_n.203, bf16[1024,3584]{1,0:T(8,128)(2,1)} %get-tuple-element.208, bf16[384,3584]{1,0:T(8,128)(2,1)S(1)} %get-tuple-element.207), kind=kOutput, calls=%fused_computation.8.clone.1 | convolution fusion | flops 939655168 | bytes 8520704 | tf_op jit(solution)/shard_map/while/body/dot_general | solution.py:20
  337.7 5.5 %fusion.31 = bf16[384,1024]{1,0:T(8,128)(2,1)S(1)} fusion(bf16[384,1024]{1,0:T(8,128)(2,1)S(1)} %get-tuple-element.196, s32[]{:T(128)S(6)} %select_n.203, bf16[1024,3584]{1,0:T(8,128)(2,1)} %get-tuple-element.208, bf16[384,3584]{1,0:T(8,128)(2,1)S(1)} %get-tuple-element.207), kind=kOutput, calls=%fused_computation.8.clone.1 | convolution fusion | flops 939655168 | bytes 8520704 | tf_op jit(solution)/shard_map/while/body/dot_general | solution.py:20
  343.9 5.5 %fusion.31 = bf16[384,1024]{1,0:T(8,128)(2,1)S(1)} fusion(bf16[384,1024]{1,0:T(8,128)(2,1)S(1)} %get-tuple-element.196, s32[]{:T(128)S(6)} %select_n.203, bf16[1024,3584]{1,0:T(8,128)(2,1)} %get-tuple-element.208, bf16[384,3584]{1,0:T(8,128)(2,1)S(1)} %get-tuple-element.207), kind=kOutput, calls=%fused_computation.8.clone.1 | convolution fusion | flops 939655168 | bytes 8520704 | tf_op jit(solution)/shard_map/while/body/dot_general | solution.py:20
  (42 shorter events, 18.1 us)
Async XLA Ops:
  10.3 10.2 %copy-start.6 = (bf16[512,8]{0,1:T(8,128)(2,1)S(1)}, bf16[512,8]{0,1:T(8,128)(2,1)}, u32[]{:S(2)}) copy-start(bf16[512,8]{0,1:T(8,128)(2,1)} %param.15) | copy-start | bytes 24580
  10.3 10.8 %copy-start.5 = (s32[512,8]{0,1:T(8,128)S(1)}, s32[512,8]{0,1:T(8,128)}, u32[]{:S(2)}) copy-start(s32[512,8]{0,1:T(8,128)} %param.14) | copy-start | bytes 49156
  10.3 10.9 %copy-start.7 = (s32[1,1,384]{2,1,0:T(1,128)S(1)}, s32[1,1,384]{2,1,0:T(1,128)}, u32[]{:S(2)}) copy-start(s32[1,1,384]{2,1,0:T(1,128)} %param.16) | copy-start | bytes 4612
  10.3 92.4 %all-to-all-start = ((bf16[16,512,224]{1,2,0:T(8,128)(2,1)}), bf16[16,512,224]{1,2,0:T(8,128)(2,1)}, u32[]{:S(2)}, u32[]{:S(2)}) async-start(bf16[16,512,224]{1,2,0:T(8,128)(2,1)} %stack.7), calls=%async_computation | async-start | bytes 7340032 | tf_op jit(solution)/shard_map/all_to_all | solution.py:43
  20.4 329.7 %reduce-scatter.4.cloned.1.call-start = ((), (), s32[]{:S(2)}) async-start(), calls=%async_computation.2 | async-start | bytes 7798784
  118.7 2.7 copy-start.3
  175.7 80.9 %collective-permute-start = (bf16[512,1792]{1,0:T(8,128)(2,1)}, bf16[512,1792]{1,0:T(8,128)(2,1)}, u32[]{:S(2)}, u32[]{:S(2)}) collective-permute-start(bf16[512,1792]{1,0:T(8,128)(2,1)} %select_convert_fusion), channel_id=1, source_target_pairs={{0,8},{1,9},{2,10},{3,11},{4,12},{5,13},{6,14},{7,15},{8,0},{9,1},... | collective-permute-start | bytes 5505032 | tf_op jit(solution)/shard_map/ppermute | solution.py:11
  260.8 1.9 copy-start
  263.9 41.3 %collective-permute-start.1 = (bf16[512,896]{1,0:T(8,128)(2,1)}, bf16[512,896]{1,0:T(8,128)(2,1)}, u32[]{:S(2)}, u32[]{:S(2)}) collective-permute-start(bf16[512,896]{1,0:T(8,128)(2,1)} %select_convert_fusion.1), channel_id=1, source_target_pairs={{0,4},{1,5},{2,6},{3,7},{4,0},{5,1},{6,2},{7,3},{8,12},{9,13},{10,... | collective-permute-start | bytes 2752520 | tf_op jit(solution)/shard_map/ppermute | solution.py:11
  307.7 1.3 copy-start.1
  309.2 13.4 %collective-permute-start.2 = (bf16[512,448]{1,0:T(8,128)(2,1)S(1)}, bf16[512,448]{1,0:T(8,128)(2,1)}, u32[]{:S(2)}, u32[]{:S(2)}) collective-permute-start(bf16[512,448]{1,0:T(8,128)(2,1)S(1)} %select_convert_fusion.2), channel_id=1, source_target_pairs={{0,2},{1,3},{2,0},{3,1},{4,6},{5,7},{6,4},{7,5},{8,10},{9,11},{10,... | collective-permute-start | bytes 1376264 | tf_op jit(solution)/shard_map/ppermute | solution.py:11
  324.7 1.0 copy-start.2
  325.8 2.6 collective-permute-start.3
  350.1 3.3 copy-start.4
Sparse Core Ops, SparseCore 0:
  137.7 86.9 reduce-scatter.3
